TPU v7x, 32 devices: a whole 2x2x4 slice. The times are simulated.
32 devices in a mesh: dp: 16 (over z, y, core), seq: 2 (over x).
Axes of the slice: x: 2, y: 2, z: 4, core: 2. Of those that a mesh axis runs over, the one named last changes fastest.
Arguments:
- latents: float32 [16, 256, 1152], P('dp', 'seq'), may hold values from -6 to 6
- condition: float32 [8, 1152], replicated, may hold values from -6 to 6
- slot_latent: int32 [16, 1], P('dp'), may hold values from 0 to 7, as said below
- slot_counts: int32 [16], P('dp'), may hold values from 0 to 1, as said below
- output_gradient: float32 [16, 256, 1152], P('dp', 'seq'), may hold values from -6 to 6
- ada_weight: float32 [1152, 6912], P(None, ('dp', 'seq')), may hold values from -0.1875 to 0.1875
- ada_bias: float32 [6912], P(('dp', 'seq')), may hold values from -1.75 to 1.75
- qkv_weight: float32 [1152, 3456], P('dp', 'seq'), may hold values from -5 to 5, as said below
- qkv_bias: float32 [3456], P('seq'), may hold values from -1.25 to 1.25
- out_weight: float32 [1152, 1152], P('dp', 'seq'), may hold values from -0.75 to 0.75
- out_bias: float32 [1152], P('seq'), may hold values from -1.25 to 1.25
- up_weight: float32 [1152, 4608], P('dp', 'seq'), may hold values from -0.1875 to 0.1875
- up_bias: float32 [4608], P('seq'), may hold values from -1.25 to 1.25
- down_weight: float32 [4608, 1152], P('dp', 'seq'), may hold values from -0.09375 to 0.09375
- down_bias: float32 [1152], P('seq'), may hold values from -1.25 to 1.25
- mean_adaw: float32 [1152, 6912], P(None, ('dp', 'seq')), may hold values from -16 to 16
- mean_adab: float32 [6912], P(('dp', 'seq')), may hold values from -16 to 16
- mean_qkvw: float32 [1152, 3456], P('dp', 'seq'), may hold values from -16 to 16
- mean_qkvb: float32 [3456], P('seq'), may hold values from -16 to 16
- mean_outw: float32 [1152, 1152], P('dp', 'seq'), may hold values from -16 to 16
- mean_outb: float32 [1152], P('seq'), may hold values from -16 to 16
- mean_upw: float32 [1152, 4608], P('dp', 'seq'), may hold values from -16 to 16
- mean_upb: float32 [4608], P('seq'), may hold values from -16 to 16
- mean_downw: float32 [4608, 1152], P('dp', 'seq'), may hold values from -16 to 16
- mean_downb: float32 [1152], P('seq'), may hold values from -16 to 16
- sqmean_adaw: float32 [1152, 6912], P(None, ('dp', 'seq')), may hold values from 0.3 to 3
- sqmean_adab: float32 [6912], P(('dp', 'seq')), may hold values from 0.3 to 3
- sqmean_qkvw: float32 [1152, 3456], P('dp', 'seq'), may hold values from 0.3 to 3
- sqmean_qkvb: float32 [3456], P('seq'), may hold values from 0.3 to 3
- sqmean_outw: float32 [1152, 1152], P('dp', 'seq'), may hold values from 0.3 to 3
- sqmean_outb: float32 [1152], P('seq'), may hold values from 0.3 to 3
- sqmean_upw: float32 [1152, 4608], P('dp', 'seq'), may hold values from 0.3 to 3
- sqmean_upb: float32 [4608], P('seq'), may hold values from 0.3 to 3
- sqmean_downw: float32 [4608, 1152], P('dp', 'seq'), may hold values from 0.3 to 3
- sqmean_downb: float32 [1152], P('seq'), may hold values from 0.3 to 3
Outputs:
- block_output: float32 [16, 256, 1152], P('dp', 'seq')
- latent_gradient: float32 [16, 256, 1152], P('dp', 'seq')
- condition_grad: float32 [8, 1152], replicated
- grad_adaw: float32 [1152, 6912], P(None, ('dp', 'seq'))
- grad_adab: float32 [6912], P(('dp', 'seq'))
- grad_qkvw: float32 [1152, 3456], P('dp', 'seq')
- grad_qkvb: float32 [3456], P('seq')
- grad_outw: float32 [1152, 1152], P('dp', 'seq')
- grad_outb: float32 [1152], P('seq')
- grad_upw: float32 [1152, 4608], P('dp', 'seq')
- grad_upb: float32 [4608], P('seq')
- grad_downw: float32 [4608, 1152], P('dp', 'seq')
- grad_downb: float32 [1152], P('seq')
- newval_adaw: float32 [1152, 6912], P(None, ('dp', 'seq'))
- newval_adab: float32 [6912], P(('dp', 'seq'))
- newval_qkvw: float32 [1152, 3456], P('dp', 'seq')
- newval_qkvb: float32 [3456], P('seq')
- newval_outw: float32 [1152, 1152], P('dp', 'seq')
- newval_outb: float32 [1152], P('seq')
- newval_upw: float32 [1152, 4608], P('dp', 'seq')
- newval_upb: float32 [4608], P('seq')
- newval_downw: float32 [4608, 1152], P('dp', 'seq')
- newval_downb: float32 [1152], P('seq')
- newmean_adaw: float32 [1152, 6912], P(None, ('dp', 'seq'))
- newmean_adab: float32 [6912], P(('dp', 'seq'))
- newmean_qkvw: float32 [1152, 3456], P('dp', 'seq')
- newmean_qkvb: float32 [3456], P('seq')
- newmean_outw: float32 [1152, 1152], P('dp', 'seq')
- newmean_outb: float32 [1152], P('seq')
- newmean_upw: float32 [1152, 4608], P('dp', 'seq')
- newmean_upb: float32 [4608], P('seq')
- newmean_downw: float32 [4608, 1152], P('dp', 'seq')
- newmean_downb: float32 [1152], P('seq')
- newsqr_adaw: float32 [1152, 6912], P(None, ('dp', 'seq'))
- newsqr_adab: float32 [6912], P(('dp', 'seq'))
- newsqr_qkvw: float32 [1152, 3456], P('dp', 'seq')
- newsqr_qkvb: float32 [3456], P('seq')
- newsqr_outw: float32 [1152, 1152], P('dp', 'seq')
- newsqr_outb: float32 [1152], P('seq')
- newsqr_upw: float32 [1152, 4608], P('dp', 'seq')
- newsqr_upb: float32 [4608], P('seq')
- newsqr_downw: float32 [4608, 1152], P('dp', 'seq')
- newsqr_downb: float32 [1152], P('seq')
Inputs may be any that keep to these rules, and one draw needn't show every extreme that they name: `slot_counts`: live slots of a group come first; the entries sum to 8; some group has all 1 slots live in every draw, some groups may have none. `slot_latent`: the live slots name every latent exactly once; entries of slots that are not live are arbitrary latents. `qkv_weight`: query and value columns have entries of order 1152^-1/2; key columns may have entries up to the ends of the range.
All inputs are finite; a program needn't handle non-finite values.
Results may differ from a plain program's by a relative error of at most 0.012.
The roundings to bfloat16 on the way count: a program that leaves them out, or rounds other values in their place, can miss the bound.
Values may be sent and summed in bfloat16 or wider, within the bound.
A program may use at most 192 MiB of HBM per device.

v0:
```python
import jax
import jax.numpy as jnp
from jax import lax
from jax.sharding import PartitionSpec as P

H = 16
HD = 72
STEP = 2
EPS_NORM = 1e-06
GELU_COEF = 0.7978845608
GELU_CUBE = 0.044715
BETA_ONE = 0.9
BETA_TWO = 0.999
LEARN_RATE = 0.05
EPS_ADAM = 1e-08


def rounded(values):
    return lax.optimization_barrier(values.astype(jnp.bfloat16)).astype(jnp.float32)


def normalize(values):
    center = values - jnp.mean(values, axis=-1, keepdims=True)
    spread = lax.rsqrt(jnp.mean(center * center, axis=-1, keepdims=True) + EPS_NORM)
    return (center * spread, spread)


def norm_back(upstream, normed, spread):
    return spread * (
        upstream
        - jnp.mean(upstream, axis=-1, keepdims=True)
        - normed * jnp.mean(upstream * normed, axis=-1, keepdims=True)
    )


def gelu_tanh(values):
    tanh_part = jnp.tanh(GELU_COEF * (values + GELU_CUBE * values * values * values))
    return 0.5 * values * (1.0 + tanh_part)


def gelu_slope(values):
    tanh_part = jnp.tanh(GELU_COEF * (values + GELU_CUBE * values * values * values))
    return 0.5 * (1.0 + tanh_part) + 0.5 * values * (1.0 - tanh_part * tanh_part) * GELU_COEF * (
        1.0 + 3.0 * GELU_CUBE * values * values
    )


def silu_slope(values):
    sigmoid_part = jax.nn.sigmoid(values)
    return sigmoid_part * (1.0 + values * (1.0 - sigmoid_part))


def adamw_step(parameter, gradient, first_mom, second):
    first_new = BETA_ONE * first_mom + (1.0 - BETA_ONE) * gradient
    second_new = BETA_TWO * second + (1.0 - BETA_TWO) * gradient * gradient
    first_hat = first_new / (1.0 - BETA_ONE**STEP)
    second_hat = second_new / (1.0 - BETA_TWO**STEP)
    return (
        parameter - LEARN_RATE * first_hat / (jnp.sqrt(second_hat) + EPS_ADAM),
        first_new,
        second_new,
    )


def collect(weight, bias):
    pieces, bias_full = (
        lax.all_gather(weight.astype(jnp.bfloat16), "seq", axis=1, tiled=True),
        lax.all_gather(bias.astype(jnp.bfloat16), "seq", axis=0, tiled=True),
    )
    return (lax.all_gather(pieces, "dp", axis=0, tiled=True), bias_full.astype(jnp.float32))


def collect_again(weight):
    pieces = lax.all_gather(weight.astype(jnp.bfloat16), "seq", axis=1, tiled=True)
    return lax.all_gather(pieces, "dp", axis=0, tiled=True)


def spread_grad(left, right):
    term = jnp.einsum("rc,rd->cd", left, right, preferred_element_type=jnp.float32)
    partial_value = lax.psum_scatter(term, "dp", scatter_dimension=0, tiled=True)
    return lax.psum_scatter(partial_value, "seq", scatter_dimension=1, tiled=True)


def on_device(
    latents,
    condition,
    slot_latent,
    slot_counts,
    output_gradient,
    ada_weight,
    ada_bias,
    qkv_weight,
    qkv_bias,
    out_weight,
    out_bias,
    up_weight,
    up_bias,
    down_weight,
    down_bias,
    mean_adaw,
    mean_adab,
    mean_qkvw,
    mean_qkvb,
    mean_outw,
    mean_outb,
    mean_upw,
    mean_upb,
    mean_downw,
    mean_downb,
    sqmean_adaw,
    sqmean_adab,
    sqmean_qkvw,
    sqmean_qkvb,
    sqmean_outw,
    sqmean_outb,
    sqmean_upw,
    sqmean_upb,
    sqmean_downw,
    sqmean_downb,
):
    slot_total, tok_dev, model_width = latents.shape
    row_count = slot_total * tok_dev
    scale = HD ** (-0.5)
    live_slots = jnp.arange(slot_total) < slot_counts[0]
    live_mask = live_slots[:, None, None]
    latent_count = condition.shape[0]
    slot_matches = (
        (slot_latent[0][:, None] == jnp.arange(latent_count)[None, :]) & live_slots[:, None]
    ).astype(jnp.float32)
    silu_cond = jax.nn.silu(condition).astype(jnp.bfloat16)
    mod_cols = jnp.dot(
        silu_cond, ada_weight.astype(jnp.bfloat16), preferred_element_type=jnp.float32
    ) + rounded(ada_bias)
    modulation = lax.all_gather(mod_cols, ("dp", "seq"), axis=1, tiled=True)
    slot_mod = jnp.dot(slot_matches, modulation, precision=lax.Precision.HIGHEST)[:, None, :]
    shift_att, scale_att, gate_att, shift_mlp, scale_mlp, gate_mlp = jnp.split(slot_mod, 6, axis=2)
    upstream = jnp.where(live_mask, output_gradient, 0.0)
    mat_qkv, vec_qkv = collect(qkv_weight, qkv_bias)
    normed_att, spread_att = normalize(latents)
    attn_in = (
        (normed_att * (1.0 + scale_att) + shift_att)
        .astype(jnp.bfloat16)
        .reshape(row_count, model_width)
    )
    qkv_all = (jnp.dot(attn_in, mat_qkv, preferred_element_type=jnp.float32) + vec_qkv).astype(
        jnp.bfloat16
    )
    queries = qkv_all[:, :model_width].reshape(slot_total, tok_dev, H, HD)
    keys_own = qkv_all[:, model_width : 2 * model_width].reshape(slot_total, tok_dev, model_width)
    values_own = qkv_all[:, 2 * model_width :].reshape(slot_total, tok_dev, model_width)
    keys_all, values_all = (
        lax.all_gather(keys_own, "seq", axis=1, tiled=True),
        lax.all_gather(values_own, "seq", axis=1, tiled=True),
    )
    keys_heads = keys_all.reshape(slot_total, -1, H, HD)
    values_heads = values_all.reshape(slot_total, -1, H, HD)
    scores = (
        jnp.einsum("sqhd,skhd->shqk", queries, keys_heads, preferred_element_type=jnp.float32)
        * scale
    )
    row_max = jnp.max(scores, axis=-1, keepdims=True)
    row_total = jnp.sum(jnp.exp(scores - row_max), axis=-1, keepdims=True)
    attn_probs = jnp.exp(scores - row_max) / row_total
    probs_b = attn_probs.astype(jnp.bfloat16)
    attended = jnp.einsum(
        "shqk,skhd->sqhd", probs_b, values_heads, preferred_element_type=jnp.float32
    )
    attended_b = attended.reshape(row_count, model_width).astype(jnp.bfloat16)
    mat_out, vec_out = collect(out_weight, out_bias)
    branch_att = (
        jnp.dot(attended_b, mat_out, preferred_element_type=jnp.float32) + vec_out
    ).reshape(slot_total, tok_dev, model_width)
    middle = latents + gate_att * branch_att
    normed_mlp, spread_mlp = normalize(middle)
    mlp_in = (
        (normed_mlp * (1.0 + scale_mlp) + shift_mlp)
        .astype(jnp.bfloat16)
        .reshape(row_count, model_width)
    )
    mat_up, vec_up = collect(up_weight, up_bias)
    hidden = jnp.dot(mlp_in, mat_up, preferred_element_type=jnp.float32) + vec_up
    activated = gelu_tanh(hidden).astype(jnp.bfloat16)
    mat_down, vec_down = collect(down_weight, down_bias)
    branch_mlp = (
        jnp.dot(activated, mat_down, preferred_element_type=jnp.float32) + vec_down
    ).reshape(slot_total, tok_dev, model_width)
    block_output = jnp.where(live_mask, middle + gate_mlp * branch_mlp, 0.0)
    mat_down = collect_again(down_weight)
    back_down = upstream * gate_mlp
    back_down_b = back_down.astype(jnp.bfloat16).reshape(row_count, model_width)
    grad_downw = spread_grad(activated, back_down_b)
    sum_downb = jnp.sum(back_down, axis=(0, 1))
    back_hidden = jnp.einsum(
        "rd,fd->rf", back_down_b, mat_down, preferred_element_type=jnp.float32
    ) * gelu_slope(hidden)
    back_hidden_b = back_hidden.astype(jnp.bfloat16)
    mat_up = collect_again(up_weight)
    grad_upw = spread_grad(mlp_in, back_hidden_b)
    sum_upb = jnp.sum(back_hidden, axis=0)
    back_mlp_in = jnp.einsum(
        "rf,cf->rc", back_hidden_b, mat_up, preferred_element_type=jnp.float32
    ).reshape(slot_total, tok_dev, model_width)
    back_middle = upstream + norm_back(back_mlp_in * (1.0 + scale_mlp), normed_mlp, spread_mlp)
    back_att = back_middle * gate_att
    back_att_b = back_att.astype(jnp.bfloat16).reshape(row_count, model_width)
    mat_out = collect_again(out_weight)
    grad_outw = spread_grad(attended_b, back_att_b)
    sum_outb = jnp.sum(back_att, axis=(0, 1))
    back_attended = jnp.einsum(
        "rd,cd->rc", back_att_b, mat_out, preferred_element_type=jnp.float32
    ).astype(jnp.bfloat16)
    back_attended = back_attended.reshape(slot_total, tok_dev, H, HD)
    back_probs = jnp.einsum(
        "sqhd,skhd->shqk", back_attended, values_heads, preferred_element_type=jnp.float32
    )
    row_delta = jnp.einsum("sqhd,sqhd->shq", back_attended.astype(jnp.float32), attended)[..., None]
    back_scores = (attn_probs * (back_probs - row_delta) * scale).astype(jnp.bfloat16)
    back_queries = jnp.einsum(
        "shqk,skhd->sqhd", back_scores, keys_heads, preferred_element_type=jnp.float32
    )
    key_terms = jnp.einsum(
        "shqk,sqhd->skhd", back_scores, queries, preferred_element_type=jnp.float32
    ).reshape(slot_total, -1, model_width)
    value_terms = jnp.einsum(
        "shqk,sqhd->skhd", probs_b, back_attended, preferred_element_type=jnp.float32
    ).reshape(slot_total, -1, model_width)
    back_keys, back_values = (
        lax.psum_scatter(key_terms, "seq", scatter_dimension=1, tiled=True),
        lax.psum_scatter(value_terms, "seq", scatter_dimension=1, tiled=True),
    )
    back_qkv = jnp.concatenate(
        [
            back_queries.reshape(row_count, model_width),
            back_keys.reshape(row_count, model_width),
            back_values.reshape(row_count, model_width),
        ],
        axis=1,
    )
    back_qkv_b = back_qkv.astype(jnp.bfloat16)
    mat_qkv = collect_again(qkv_weight)
    grad_qkvw = spread_grad(attn_in, back_qkv_b)
    sum_qkvb = jnp.sum(back_qkv, axis=0)
    back_attn_in = jnp.einsum(
        "rd,cd->rc", back_qkv_b, mat_qkv, preferred_element_type=jnp.float32
    ).reshape(slot_total, tok_dev, model_width)
    latent_gradient = jnp.where(
        live_mask,
        back_middle + norm_back(back_attn_in * (1.0 + scale_att), normed_att, spread_att),
        0.0,
    )
    slot_modgrad = jnp.concatenate(
        [
            jnp.sum(back_attn_in, axis=1),
            jnp.sum(back_attn_in * normed_att, axis=1),
            jnp.sum(back_middle * branch_att, axis=1),
            jnp.sum(back_mlp_in, axis=1),
            jnp.sum(back_mlp_in * normed_mlp, axis=1),
            jnp.sum(upstream * branch_mlp, axis=1),
        ],
        axis=1,
    )
    modgrad_table = jnp.dot(slot_matches.T, slot_modgrad, precision=lax.Precision.HIGHEST)
    modgrad_cols = lax.psum_scatter(modgrad_table, ("dp", "seq"), scatter_dimension=1, tiled=True)
    grad_adaw = jnp.dot(
        rounded(jax.nn.silu(condition)).T, modgrad_cols, precision=lax.Precision.HIGHEST
    )
    grad_adab = jnp.sum(modgrad_cols, axis=0)
    cond_term = jnp.dot(modgrad_cols, rounded(ada_weight).T, precision=lax.Precision.HIGHEST)
    cond_sum, total_qkvb, total_outb, total_upb, total_downb = lax.psum(
        (cond_term, sum_qkvb, sum_outb, sum_upb, sum_downb), ("dp", "seq")
    )
    condition_grad = cond_sum * silu_slope(condition)
    seq_index = lax.axis_index("seq")

    def own_part(full_sum, local_bias):
        length = local_bias.shape[0]
        return lax.dynamic_slice_in_dim(full_sum, seq_index * length, length)

    grad_qkvb = own_part(total_qkvb, qkv_bias)
    grad_outb = own_part(total_outb, out_bias)
    grad_upb = own_part(total_upb, up_bias)
    grad_downb = own_part(total_downb, down_bias)
    grads_all = (
        grad_adaw,
        grad_adab,
        grad_qkvw,
        grad_qkvb,
        grad_outw,
        grad_outb,
        grad_upw,
        grad_upb,
        grad_downw,
        grad_downb,
    )
    params_all = (
        ada_weight,
        ada_bias,
        qkv_weight,
        qkv_bias,
        out_weight,
        out_bias,
        up_weight,
        up_bias,
        down_weight,
        down_bias,
    )
    means_all = (
        mean_adaw,
        mean_adab,
        mean_qkvw,
        mean_qkvb,
        mean_outw,
        mean_outb,
        mean_upw,
        mean_upb,
        mean_downw,
        mean_downb,
    )
    squares_all = (
        sqmean_adaw,
        sqmean_adab,
        sqmean_qkvw,
        sqmean_qkvb,
        sqmean_outw,
        sqmean_outb,
        sqmean_upw,
        sqmean_upb,
        sqmean_downw,
        sqmean_downb,
    )
    updates = [
        adamw_step(p_item, g_item, m_item, v_item)
        for p_item, g_item, m_item, v_item in zip(params_all, grads_all, means_all, squares_all)
    ]
    newvals = tuple((entry[0] for entry in updates))
    newmeans = tuple((entry[1] for entry in updates))
    newsqrs = tuple((entry[2] for entry in updates))
    return (
        (block_output, latent_gradient, condition_grad) + grads_all + newvals + newmeans + newsqrs
    )


def solution(mesh):
    return jax.shard_map(
        on_device,
        mesh=mesh,
        in_specs=(
            P("dp", "seq", None),
            P(),
            P("dp", None),
            P("dp"),
            P("dp", "seq", None),
            P(None, ("dp", "seq")),
            P(("dp", "seq")),
            P("dp", "seq"),
            P("seq"),
            P("dp", "seq"),
            P("seq"),
            P("dp", "seq"),
            P("seq"),
            P("dp", "seq"),
            P("seq"),
            P(None, ("dp", "seq")),
            P(("dp", "seq")),
            P("dp", "seq"),
            P("seq"),
            P("dp", "seq"),
            P("seq"),
            P("dp", "seq"),
            P("seq"),
            P("dp", "seq"),
            P("seq"),
            P(None, ("dp", "seq")),
            P(("dp", "seq")),
            P("dp", "seq"),
            P("seq"),
            P("dp", "seq"),
            P("seq"),
            P("dp", "seq"),
            P("seq"),
            P("dp", "seq"),
            P("seq"),
        ),
        out_specs=(
            P("dp", "seq", None),
            P("dp", "seq", None),
            P(),
            P(None, ("dp", "seq")),
            P(("dp", "seq")),
            P("dp", "seq"),
            P("seq"),
            P("dp", "seq"),
            P("seq"),
            P("dp", "seq"),
            P("seq"),
            P("dp", "seq"),
            P("seq"),
            P(None, ("dp", "seq")),
            P(("dp", "seq")),
            P("dp", "seq"),
            P("seq"),
            P("dp", "seq"),
            P("seq"),
            P("dp", "seq"),
            P("seq"),
            P("dp", "seq"),
            P("seq"),
            P(None, ("dp", "seq")),
            P(("dp", "seq")),
            P("dp", "seq"),
            P("seq"),
            P("dp", "seq"),
            P("seq"),
            P("dp", "seq"),
            P("seq"),
            P("dp", "seq"),
            P("seq"),
            P(None, ("dp", "seq")),
            P(("dp", "seq")),
            P("dp", "seq"),
            P("seq"),
            P("dp", "seq"),
            P("seq"),
            P("dp", "seq"),
            P("seq"),
            P("dp", "seq"),
            P("seq"),
        ),
        check_vma=False,
    )
```

profile of v0, /device:TPU:0, one launch (start us, length us, event | category | flops | bytes accessed | tf_op | source)
XLA Modules:
  0.0 1488.1 jit_solution(5045543389649155626)
XLA Ops:
  8.4 10.0 all-gather.3
  20.1 5.4 all-gather.4
  26.6 8.7 all_gather.62
  37.1 70.0 %all-gather.2 = f32[32,216,8]{1,2,0:T(8,128)S(1)} all-gather(f32[1,216,8]{1,2,0:T(8,128)S(1)} %fusion.10), channel_id=1, replica_groups=mesh['dp'=16,'seq'=2] {'dp','seq'}, dimensions={0}, use_global_device_ids=true | all-gather | bytes 228096 | tf_op jit(solution)/shard_map/all_gather | solution.py:134
  111.4 7.3 all-reduce.7
  118.7 4.4 all-gather.5
  125.1 4.8 fusion.1
  129.9 7.7 all-gather
  139.6 8.0 all-gather.1
  147.8 2.2 fusion.94
  152.9 3.3 fusion.92
  157.0 71.1 %all-gather.16.cloned.1.call-done = bf16[1152,4608]{1,0:T(8,128)(2,1)} async-done(((bf16[72,4608]{1,0:T(8,128)(2,1)}), bf16[1152,4608]{1,0:T(8,128)(2,1)}) %all-gather.16.cloned.1.call-update) | async-done | bytes 10616848 | tf_op jit(solution)/shard_map/all_gather | solution.py:70
  228.0 5.9 convolution_add_fusion
  233.9 8.7 fusion.45
  242.7 211.9 %reduce-scatter.30.cloned.1.call-done = f32[288,1152]{1,0:T(8,128)} async-done(((f32[4608,1152]{1,0:T(8,128)}), f32[288,1152]{1,0:T(8,128)}) %reduce-scatter.30.cloned.1.call-update) | async-done | bytes 1327120 | tf_op jit(solution)/shard_map/reduce_scatter | solution.py:80
  454.7 3.1 copy.116
  457.8 27.5 %reduce-scatter.36.cloned.1.call-done = f32[576,288]{1,0:T(8,128)} async-done(((f32[1152,288]{1,0:T(8,128)}), f32[576,288]{1,0:T(8,128)}) %reduce-scatter.36.cloned.1.call-update) | async-done | bytes 663568
  485.4 2.3 copy.117
  487.7 3.6 divide_subtract_fusion.1
  491.3 10.8 all-gather.6
  502.1 1.4 copy.100
  503.6 2.8 reshape.400
  507.9 87.0 %all-gather.18.cloned.1.call-done = bf16[4608,1152]{1,0:T(8,128)(2,1)} async-done(((bf16[288,1152]{1,0:T(8,128)(2,1)}), bf16[4608,1152]{1,0:T(8,128)(2,1)}) %all-gather.18.cloned.1.call-update) | async-done | bytes 10616848 | tf_op jit(solution)/shard_map/all_gather | solution.py:70
  594.9 8.7 fusion.95
  603.7 8.6 fusion.17
  613.0 3.8 multiply_reduce_fusion.4
  620.3 2.7 multiply_convert_fusion.1
  625.1 15.3 %reduce-scatter.24.cloned.1.call-done = f32[1,128,1152]{1,2,0:T(8,128)} async-done(((f32[1,256,1152]{1,2,0:T(8,128)}), f32[1,128,1152]{1,2,0:T(8,128)}) %reduce-scatter.24.cloned.1.call-update) | async-done | bytes 589840 | tf_op jit(solution)/shard_map/reduce_scatter | solution.py:229
  640.4 24.1 %reduce-scatter.22.cloned.1.call-done = f32[1,128,1152]{1,2,0:T(8,128)} async-done(((f32[1,256,1152]{1,2,0:T(8,128)}), f32[1,128,1152]{1,2,0:T(8,128)}) %reduce-scatter.22.cloned.1.call-update) | async-done | bytes 589840 | tf_op jit(solution)/shard_map/reduce_scatter | solution.py:228
  664.6 6.8 fusion.19
  673.3 3.2 fusion.42
  677.5 9.1 fusion.71
  686.7 11.5 fusion.29
  700.4 97.5 %all-reduce.11.cloned.1.call-done = f32[8,6912]{1,0:T(8,128)} async-done(((f32[8,6912]{1,0:T(8,128)}), f32[8,6912]{1,0:T(8,128)}) %all-reduce.11.cloned.1.call-update) | async-done | bytes 221200
  797.9 2.1 fusion.52
  800.0 80.8 %reduce-scatter.40.cloned.1.call-done = f32[72,1152]{1,0:T(8,128)} async-done(((f32[1152,1152]{1,0:T(8,128)}), f32[72,1152]{1,0:T(8,128)}) %reduce-scatter.40.cloned.1.call-update) | async-done | bytes 331792
  880.8 2.0 copy.114
  883.0 171.3 %reduce-scatter.38.cloned.1.call-done = f32[72,3456]{1,0:T(8,128)} async-done(((f32[1152,3456]{1,0:T(8,128)}), f32[72,3456]{1,0:T(8,128)}) %reduce-scatter.38.cloned.1.call-update) | async-done | bytes 995344
  1054.3 3.0 copy.112
  1059.4 211.5 %reduce-scatter.26.cloned.1.call-done = f32[72,4608]{1,0:T(8,128)} async-done(((f32[1152,4608]{1,0:T(8,128)}), f32[72,4608]{1,0:T(8,128)}) %reduce-scatter.26.cloned.1.call-update) | async-done | bytes 1327120 | tf_op jit(solution)/shard_map/reduce_scatter | solution.py:80
  1271.7 4.9 divide_subtract_fusion
  1276.6 125.8 %all-reduce.13.cloned.1.call-done = (f32[8,1152]{1,0:T(8,128)}, f32[3456]{0:T(1024)}, f32[1152]{0:T(1024)}, f32[4608]{0:T(1024)}, f32[1152]{0:T(1024)}) async-done(((f32[8,1152]{1,0:T(8,128)}, f32[3456]{0:T(1024)}, f32[1152]{0:T(1024)}, f32[4608]{0:T(1024)}, f32[1152]{0:T(1024)}), (f32[8,1152]{1,0:T(8,128)}, f32[3456]{0:T(1024)}, f32[1152]{0:T(1024)}, f32[4608]{0:T(1024)}, ...) | async-done | bytes 78352 | tf_op jit(solution)/shard_map/psum | solution.py:269
  1409.5 12.6 reduce-scatter.34.cloned.1.call-done
  1424.1 28.4 %reduce-scatter.32.cloned.1.call-done = f32[1728,72]{1,0:T(8,128)} async-done(((f32[3456,72]{1,0:T(8,128)}), f32[1728,72]{1,0:T(8,128)}) %reduce-scatter.32.cloned.1.call-update) | async-done | bytes 497680
  1452.5 1.6 copy.113
  1454.1 2.7 divide_subtract_fusion.3
  1456.9 21.8 %reduce-scatter.28.cloned.1.call-done = f32[72,2304]{1,0:T(8,128)} async-done(((f32[72,4608]{1,0:T(8,128)}), f32[72,2304]{1,0:T(8,128)}) %reduce-scatter.28.cloned.1.call-update) | async-done | bytes 663568 | tf_op jit(solution)/shard_map/reduce_scatter | solution.py:81
  1478.7 2.6 divide_subtract_fusion.2
  (288 shorter events, 39.7 us)
Async XLA Ops:
  7.2 117.8 %all-gather.12.cloned.1.call-start = ((), (), s32[]{:S(2)}) async-start(), calls=%async_computation.10 | async-start | bytes 8460288 | tf_op jit(solution)/shard_map/all_gather | solution.py:70
  20.0 132.9 %all-gather.14.cloned.1.call-start = ((), (), s32[]{:S(2)}) async-start(), calls=%async_computation.11 | async-start | bytes 2820096 | tf_op jit(solution)/shard_map/all_gather | solution.py:70
  26.4 201.6 %all-gather.16.cloned.1.call-start = ((), (), s32[]{:S(2)}) async-start(), calls=%async_computation.12 | async-start | bytes 11280384 | tf_op jit(solution)/shard_map/all_gather | solution.py:70
  26.5 82.2 %copy-start.62 = (f32[576]{0:T(1024)S(1)}, f32[576]{0:T(1024)}, u32[]{:S(2)}) copy-start(f32[576]{0:T(1024)} %param.45) | copy-start | bytes 6916
  26.6 82.2 %copy-start.84 = (u32[32]{0:T(128)S(1)}, u32[32]{0:T(128)}, u32[]{:S(2)}) copy-start(u32[32]{0:T(128)} %constant.88) | copy-start | bytes 388
  26.6 84.1 %copy-start.64 = (f32[576]{0:T(1024)S(1)}, f32[576]{0:T(1024)}, u32[]{:S(2)}) copy-start(f32[576]{0:T(1024)} %param.49) | copy-start | bytes 6916
  26.6 92.1 %copy-start.43 = (f32[2304]{0:T(1024)S(1)}, f32[2304]{0:T(1024)}, u32[]{:S(2)}) copy-start(f32[2304]{0:T(1024)} %param.47) | copy-start | bytes 27652
  35.3 88.5 %copy-start = (f32[1,128,1152]{2,1,0:T(8,128)S(1)}, f32[1,128,1152]{2,1,0:T(8,128)}, u32[]{:S(2)}) copy-start(f32[1,128,1152]{2,1,0:T(8,128)} %param.35) | copy-start | bytes 1769476
  35.3 419.3 %reduce-scatter.30.cloned.1.call-start = ((), (), s32[]{:S(2)}) async-start(), calls=%async_computation.18 | async-start | bytes 22560768 | tf_op jit(solution)/shard_map/reduce_scatter | solution.py:80
  242.7 242.7 %reduce-scatter.36.cloned.1.call-start = ((), (), s32[]{:S(2)}) async-start(), calls=%async_computation.21 | async-start | bytes 2654208
  457.8 137.1 %all-gather.18.cloned.1.call-start = ((), (), s32[]{:S(2)}) async-start(), calls=%async_computation.13 | async-start | bytes 11280384 | tf_op jit(solution)/shard_map/all_gather | solution.py:70
  506.4 134.0 %reduce-scatter.24.cloned.1.call-start = ((), (), s32[]{:S(2)}) async-start(), calls=%async_computation.15 | async-start | bytes 1769472 | tf_op jit(solution)/shard_map/reduce_scatter | solution.py:229
  620.2 44.3 %reduce-scatter.22.cloned.1.call-start = ((), (), s32[]{:S(2)}) async-start(), calls=%async_computation.14 | async-start | bytes 1769472 | tf_op jit(solution)/shard_map/reduce_scatter | solution.py:228
  624.5 173.3 %all-reduce.11.cloned.1.call-start = ((), (), s32[]{:S(2)}) async-start(), calls=%async_computation.22 | async-start | bytes 442368
  673.0 207.8 %reduce-scatter.40.cloned.1.call-start = ((), (), s32[]{:S(2)}) async-start(), calls=%async_computation.24 | async-start | bytes 5640192
  676.5 377.8 %reduce-scatter.38.cloned.1.call-start = ((), (), s32[]{:S(2)}) async-start(), calls=%async_computation.23 | async-start | bytes 16920576
  686.7 584.2 %reduce-scatter.26.cloned.1.call-start = ((), (), s32[]{:S(2)}) async-start(), calls=%async_computation.16 | async-start | bytes 22560768 | tf_op jit(solution)/shard_map/reduce_scatter | solution.py:80
  698.2 704.2 %all-reduce.13.cloned.1.call-start = ((), (), s32[]{:S(2)}) async-start(), calls=%async_computation.25 | async-start | bytes 180224 | tf_op jit(solution)/shard_map/psum | solution.py:269
  799.9 622.1 %reduce-scatter.34.cloned.1.call-start = ((), (), s32[]{:S(2)}) async-start(), calls=%async_computation.20 | async-start | bytes 884736
  882.9 174.6 %copy-start.82 = (f32[128]{0:T(128)S(1)}, f32[128]{0:T(128)}, u32[]{:S(2)}) copy-start(f32[128]{0:T(128)} %get-tuple-element.46) | copy-start | bytes 1540
  882.9 174.6 %copy-start.83 = (f32[128]{0:T(128)S(1)}, f32[128]{0:T(128)}, u32[]{:S(2)}) copy-start(f32[128]{0:T(128)} %get-tuple-element.54) | copy-start | bytes 1540
  882.9 174.6 %copy-start.57 = (f32[128]{0:T(128)S(1)}, f32[128]{0:T(128)}, u32[]{:S(2)}) copy-start(f32[128]{0:T(128)} %copy-done.55) | copy-start | bytes 1540
  882.9 174.6 %copy-start.61 = (f32[128]{0:T(128)S(1)}, f32[128]{0:T(128)}, u32[]{:S(2)}) copy-start(f32[128]{0:T(128)} %copy-done.59) | copy-start | bytes 1540
  882.9 569.6 %reduce-scatter.32.cloned.1.call-start = ((), (), s32[]{:S(2)}) async-start(), calls=%async_computation.19 | async-start | bytes 2654208
  1057.3 213.6 %copy-start.79 = (f32[216]{0:T(256)S(1)}, f32[216]{0:T(256)}, u32[]{:S(2)}) copy-start(f32[216]{0:T(256)} %param.41) | copy-start | bytes 2596
  1057.3 213.6 %copy-start.80 = (f32[216]{0:T(256)S(1)}, f32[216]{0:T(256)}, u32[]{:S(2)}) copy-start(f32[216]{0:T(256)} %param.51) | copy-start | bytes 2596
  1057.3 213.6 %copy-start.81 = (f32[216]{0:T(256)S(1)}, f32[216]{0:T(256)}, u32[]{:S(2)}) copy-start(f32[216]{0:T(256)} %param.61) | copy-start | bytes 2596
  1057.3 214.2 %copy-start.14 = (f32[1152,216]{0,1:T(8,128)S(1)}, f32[1152,216]{0,1:T(8,128)}, u32[]{:S(2)}) copy-start(f32[1152,216]{0,1:T(8,128)} %param.40) | copy-start | bytes 2985988
  1057.3 214.2 %copy-start.36 = (bf16[8,1152]{1,0:T(8,128)(2,1)S(1)}, bf16[8,1152]{1,0:T(8,128)(2,1)}, u32[]{:S(2)}) copy-start(bf16[8,1152]{1,0:T(8,128)(2,1)} %copy-done.35) | copy-start | bytes 55300
  1057.4 421.3 %reduce-scatter.28.cloned.1.call-start = ((), (), s32[]{:S(2)}) async-start(), calls=%async_computation.17 | async-start | bytes 1990656 | tf_op jit(solution)/shard_map/reduce_scatter | solution.py:81
  1059.4 217.2 %copy-start.73 = (f32[216]{0:T(256)}, f32[216]{0:T(256)S(1)}, u32[]{:S(2)}) copy-start(f32[216]{0:T(256)S(1)} %dynamic-slice_reduce_fusion) | copy-start | bytes 2596
  1271.5 130.9 %copy-start.63 = (f32[576]{0:T(1024)S(1)}, f32[576]{0:T(1024)}, u32[]{:S(2)}) copy-start(f32[576]{0:T(1024)} %param.45) | copy-start | bytes 6916
  1271.5 130.9 %copy-start.74 = (f32[576]{0:T(1024)S(1)}, f32[576]{0:T(1024)}, u32[]{:S(2)}) copy-start(f32[576]{0:T(1024)} %param.55) | copy-start | bytes 6916
  1271.5 130.9 %copy-start.75 = (f32[576]{0:T(1024)S(1)}, f32[576]{0:T(1024)}, u32[]{:S(2)}) copy-start(f32[576]{0:T(1024)} %param.65) | copy-start | bytes 6916
  1271.5 132.3 %copy-start.65 = (f32[576]{0:T(1024)S(1)}, f32[576]{0:T(1024)}, u32[]{:S(2)}) copy-start(f32[576]{0:T(1024)} %param.49) | copy-start | bytes 6916
  1271.6 132.3 %copy-start.76 = (f32[576]{0:T(1024)S(1)}, f32[576]{0:T(1024)}, u32[]{:S(2)}) copy-start(f32[576]{0:T(1024)} %param.59) | copy-start | bytes 6916
  1271.6 132.2 %copy-start.77 = (f32[576]{0:T(1024)S(1)}, f32[576]{0:T(1024)}, u32[]{:S(2)}) copy-start(f32[576]{0:T(1024)} %param.69) | copy-start | bytes 6916
  1271.6 133.6 %copy-start.51 = (f32[1728]{0:T(1024)S(1)}, f32[1728]{0:T(1024)}, u32[]{:S(2)}) copy-start(f32[1728]{0:T(1024)} %param.43) | copy-start | bytes 20740
  1271.6 133.6 %copy-start.71 = (f32[1728]{0:T(1024)S(1)}, f32[1728]{0:T(1024)}, u32[]{:S(2)}) copy-start(f32[1728]{0:T(1024)} %param.53) | copy-start | bytes 20740
  1271.6 133.6 %copy-start.72 = (f32[1728]{0:T(1024)S(1)}, f32[1728]{0:T(1024)}, u32[]{:S(2)}) copy-start(f32[1728]{0:T(1024)} %param.63) | copy-start | bytes 20740
  1271.6 135.0 %copy-start.44 = (f32[2304]{0:T(1024)S(1)}, f32[2304]{0:T(1024)}, u32[]{:S(2)}) copy-start(f32[2304]{0:T(1024)} %param.47) | copy-start | bytes 27652
  1271.6 135.0 %copy-start.66 = (f32[2304]{0:T(1024)S(1)}, f32[2304]{0:T(1024)}, u32[]{:S(2)}) copy-start(f32[2304]{0:T(1024)} %param.57) | copy-start | bytes 27652
  1271.6 135.0 %copy-start.67 = (f32[2304]{0:T(1024)S(1)}, f32[2304]{0:T(1024)}, u32[]{:S(2)}) copy-start(f32[2304]{0:T(1024)} %param.67) | copy-start | bytes 27652
  1271.7 136.4 %copy-start.38 = (f32[8,1152]{1,0:T(8,128)S(1)}, f32[8,1152]{1,0:T(8,128)}, u32[]{:S(2)}) copy-start(f32[8,1152]{1,0:T(8,128)} %param.36) | copy-start | bytes 110596
  1271.7 151.5 %copy-start.26 = (f32[72,576]{1,0:T(8,128)S(1)}, f32[72,576]{1,0:T(8,128)}, u32[]{:S(2)}) copy-start(f32[72,576]{1,0:T(8,128)} %param.44) | copy-start | bytes 497668
  1271.7 151.5 %copy-start.33 = (f32[72,576]{1,0:T(8,128)S(1)}, f32[72,576]{1,0:T(8,128)}, u32[]{:S(2)}) copy-start(f32[72,576]{1,0:T(8,128)} %param.54) | copy-start | bytes 497668
  1271.7 151.5 %copy-start.34 = (f32[72,576]{1,0:T(8,128)S(1)}, f32[72,576]{1,0:T(8,128)}, u32[]{:S(2)}) copy-start(f32[72,576]{1,0:T(8,128)} %param.64) | copy-start | bytes 497668
  1276.6 177.6 %copy-start.23 = (f32[72,1728]{1,0:T(8,128)S(1)}, f32[72,1728]{1,0:T(8,128)}, u32[]{:S(2)}) copy-start(f32[72,1728]{1,0:T(8,128)} %param.42) | copy-start | bytes 1492996
  (56 other events, 706.0 us)
Sparse Core Ops, SparseCore 0:
  20.1 73.9 all-gather.11
  96.8 41.6 all-gather.13
  140.8 87.1 all-gather.15
  242.8 211.8 reduce-scatter.29
  457.9 27.4 reduce-scatter.35
  506.5 88.3 all-gather.17
  620.3 20.0 reduce-scatter.23
  642.6 21.8 reduce-scatter.21
  673.1 124.6 all-reduce.10
  801.7 79.0 reduce-scatter.39
  885.0 169.3 reduce-scatter.37
  1058.3 212.5 reduce-scatter.25
  1279.0 123.3 all-reduce.12
  1405.1 16.9 reduce-scatter.33
  1424.2 28.3 reduce-scatter.31
  1455.2 23.4 reduce-scatter.27
where the time goes:
time: 1490 us
  waiting for transfers between devices  1190 us (80%)
  blocking collectives  132 us (9%)
  matrix products  92 us (6%)
  local copies, waits for them, and re-layouts  30.4 us (2%)
  other arithmetic  27.4 us (2%)
  between operations  18 us (1%)
    reduce_scatter x2, waiting for transfers between devices, spread_grad(): lax.psum_scatter(term, 'dp', scatter_dimension=0, tiled=True)  423 us
    unnamed x22, waiting for transfers between devices  418 us
    all_gather x4, waiting for transfers between devices, collect(): lax.all_gather(pieces, 'dp', axis=0, tiled=True)  158 us
    psum x1, waiting for transfers between devices, on_device(): lax.psum((cond_term, sum_qkvb, sum_outb, sum_upb, sum_downb), ('dp', 'seq'))  126 us
    all_gather x1, blocking collectives, on_device(): modulation = lax.all_gather(mod_cols, ('dp', 'seq'), axis=1, tiled=True)  70 us
    all_gather x4, blocking collectives, collect(): lax.all_gather(weight.astype(jnp.bfloat16), 'seq', axis=1, tiled=True)  34.8 us
    dot_general x4, matrix products, spread_grad(): jnp.einsum('rc,rd->cd', left, right, preferred_element_type=jnp.float32)  32.5 us
  transfers between devices with their start and end apart: 16, of which 14 were waited for; matrix products, arithmetic and copies ran while one was open for 5% of the time, Pallas kernels for 0%

commit v1 on v0

--- a/solution.py
+++ b/solution.py
@@ -267,7 +267,7 @@
     grad_adab = jnp.sum(modgrad_cols, axis=0)
     cond_term = jnp.dot(modgrad_cols, rounded(ada_weight).T, precision=lax.Precision.HIGHEST)
     cond_sum, total_qkvb, total_outb, total_upb, total_downb = lax.psum(
-        (cond_term, sum_qkvb, sum_outb, sum_upb, sum_downb), ("dp", "seq")
+        lax.psum((cond_term, sum_qkvb, sum_outb, sum_upb, sum_downb), "seq"), "dp"
     )
     condition_grad = cond_sum * silu_slope(condition)
     seq_index = lax.axis_index("seq")

time: 1490 us -> 1490 us (level)
  waiting for transfers between devices: 1190 us -> 1170 us
    psum x1 -> x2, waiting for transfers between devices: 126 us -> 86 us  [the longest x1 86 us: on_device(): lax.psum(lax.psum((cond_term, sum_qkvb, sum_outb, sum_upb, sum_downb), 's...]
    unnamed x22 -> x23, waiting for transfers between devices: 418 us -> 443 us
  transfers between devices with their start and end apart: 16 -> 17, of which waited for: 14 -> 14; matrix products, arithmetic and copies ran while one was open for 5% -> 5% of each run, Pallas kernels for 0% -> 0%
where the time goes in v1:
time: 1490 us; the launch traced here: 1480 us
  waiting for transfers between devices  1170 us (79%)
  blocking collectives  132 us (9%)
  matrix products  92.9 us (6%)
  local copies, waits for them, and re-layouts  32.5 us (2%)
  other arithmetic  31.1 us (2%)
  between operations  17.9 us (1%)
    unnamed x23, waiting for transfers between devices  443 us
    reduce_scatter x2, waiting for transfers between devices, spread_grad(): lax.psum_scatter(term, 'dp', scatter_dimension=0, tiled=True)  424 us
    all_gather x4, waiting for transfers between devices, collect(): lax.all_gather(pieces, 'dp', axis=0, tiled=True)  158 us
    psum x1, waiting for transfers between devices, on_device(): lax.psum(lax.psum((cond_term, sum_qkvb, sum_outb, sum_upb, sum_downb), 's...  86 us
    all_gather x1, blocking collectives, on_device(): modulation = lax.all_gather(mod_cols, ('dp', 'seq'), axis=1, tiled=True)  70 us
    all_gather x4, blocking collectives, collect(): lax.all_gather(weight.astype(jnp.bfloat16), 'seq', axis=1, tiled=True)  34.9 us
    dot_general x4, matrix products, spread_grad(): jnp.einsum('rc,rd->cd', left, right, preferred_element_type=jnp.float32)  33.3 us
  transfers between devices with their start and end apart: 17, of which 14 were waited for; matrix products, arithmetic and copies ran while one was open for 5% of the time, Pallas kernels for 0%

profile of v1, /device:TPU:0, one launch (start us, length us, event | category | flops | bytes accessed | tf_op | source)
XLA Modules:
  0.0 1479.4 jit_solution(5996209003588449208)
XLA Ops:
  8.4 10.0 all-gather.3
  20.1 5.4 all-gather.4
  26.6 8.7 all_gather.62
  37.1 70.0 %all-gather.2 = f32[32,216,8]{1,2,0:T(8,128)S(1)} all-gather(f32[1,216,8]{1,2,0:T(8,128)S(1)} %fusion.10), channel_id=1, replica_groups=mesh['dp'=16,'seq'=2] {'dp','seq'}, dimensions={0}, use_global_device_ids=true | all-gather | bytes 228096 | tf_op jit(solution)/shard_map/all_gather | solution.py:134
  111.4 7.3 all-reduce.8
  118.7 4.4 all-gather.5
  125.1 4.8 fusion.1
  129.9 7.7 all-gather
  139.6 8.0 all-gather.1
  147.8 2.2 fusion.94
  152.9 3.3 fusion.92
  157.0 71.1 %all-gather.16.cloned.1.call-done = bf16[1152,4608]{1,0:T(8,128)(2,1)} async-done(((bf16[72,4608]{1,0:T(8,128)(2,1)}), bf16[1152,4608]{1,0:T(8,128)(2,1)}) %all-gather.16.cloned.1.call-update) | async-done | bytes 10616848 | tf_op jit(solution)/shard_map/all_gather | solution.py:70
  228.0 5.9 convolution_add_fusion
  233.9 8.7 fusion.45
  242.7 211.9 %reduce-scatter.30.cloned.1.call-done = f32[288,1152]{1,0:T(8,128)} async-done(((f32[4608,1152]{1,0:T(8,128)}), f32[288,1152]{1,0:T(8,128)}) %reduce-scatter.30.cloned.1.call-update) | async-done | bytes 1327120 | tf_op jit(solution)/shard_map/reduce_scatter | solution.py:80
  454.7 3.1 copy.116
  457.8 27.5 %reduce-scatter.36.cloned.1.call-done = f32[576,288]{1,0:T(8,128)} async-done(((f32[1152,288]{1,0:T(8,128)}), f32[576,288]{1,0:T(8,128)}) %reduce-scatter.36.cloned.1.call-update) | async-done | bytes 663568
  485.3 2.3 copy.117
  487.7 3.6 divide_subtract_fusion.1
  491.3 10.8 all-gather.6
  503.5 2.8 reshape.400
  507.9 87.0 %all-gather.18.cloned.1.call-done = bf16[4608,1152]{1,0:T(8,128)(2,1)} async-done(((bf16[288,1152]{1,0:T(8,128)(2,1)}), bf16[4608,1152]{1,0:T(8,128)(2,1)}) %all-gather.18.cloned.1.call-update) | async-done | bytes 10616848 | tf_op jit(solution)/shard_map/all_gather | solution.py:70
  594.9 8.7 fusion.95
  603.7 8.6 fusion.17
  613.0 3.8 multiply_reduce_fusion.4
  620.3 2.7 multiply_convert_fusion.1
  625.5 14.8 %reduce-scatter.24.cloned.1.call-done = f32[1,128,1152]{1,2,0:T(8,128)} async-done(((f32[1,256,1152]{1,2,0:T(8,128)}), f32[1,128,1152]{1,2,0:T(8,128)}) %reduce-scatter.24.cloned.1.call-update) | async-done | bytes 589840 | tf_op jit(solution)/shard_map/reduce_scatter | solution.py:229
  640.3 24.1 %reduce-scatter.22.cloned.1.call-done = f32[1,128,1152]{1,2,0:T(8,128)} async-done(((f32[1,256,1152]{1,2,0:T(8,128)}), f32[1,128,1152]{1,2,0:T(8,128)}) %reduce-scatter.22.cloned.1.call-update) | async-done | bytes 589840 | tf_op jit(solution)/shard_map/reduce_scatter | solution.py:228
  664.5 6.8 fusion.19
  678.8 2.2 fusion.8
  681.0 122.4 %all-reduce.13.cloned.1.call-done = f32[8,6912]{1,0:T(8,128)} async-done(((f32[8,6912]{1,0:T(8,128)}), f32[8,6912]{1,0:T(8,128)}) %all-reduce.13.cloned.1.call-update) | async-done | bytes 221200
  803.4 2.1 fusion.52
  805.5 4.1 fusion.42
  809.7 9.1 fusion.71
  819.5 11.4 fusion.29
  831.5 81.3 %reduce-scatter.40.cloned.1.call-done = f32[72,1152]{1,0:T(8,128)} async-done(((f32[1152,1152]{1,0:T(8,128)}), f32[72,1152]{1,0:T(8,128)}) %reduce-scatter.40.cloned.1.call-update) | async-done | bytes 331792
  912.8 2.0 copy.114
  915.0 171.4 %reduce-scatter.38.cloned.1.call-done = f32[72,3456]{1,0:T(8,128)} async-done(((f32[1152,3456]{1,0:T(8,128)}), f32[72,3456]{1,0:T(8,128)}) %reduce-scatter.38.cloned.1.call-update) | async-done | bytes 995344
  1086.4 3.0 copy.112
  1091.5 211.7 %reduce-scatter.26.cloned.1.call-done = f32[72,4608]{1,0:T(8,128)} async-done(((f32[1152,4608]{1,0:T(8,128)}), f32[72,4608]{1,0:T(8,128)}) %reduce-scatter.26.cloned.1.call-update) | async-done | bytes 1327120 | tf_op jit(solution)/shard_map/reduce_scatter | solution.py:80
  1304.0 4.9 divide_subtract_fusion
  1308.9 86.0 %all-reduce.15.cloned.1.call-done = (f32[8,1152]{1,0:T(8,128)}, f32[3456]{0:T(1024)}, f32[1152]{0:T(1024)}, f32[4608]{0:T(1024)}, f32[1152]{0:T(1024)}) async-done(((f32[8,1152]{1,0:T(8,128)}, f32[3456]{0:T(1024)}, f32[1152]{0:T(1024)}, f32[4608]{0:T(1024)}, f32[1152]{0:T(1024)}), (f32[8,1152]{1,0:T(8,128)}, f32[3456]{0:T(1024)}, f32[1152]{0:T(1024)}, f32[4608]{0:T(1024)}, ...) | async-done | bytes 78352 | tf_op jit(solution)/shard_map/psum | solution.py:269
  1402.0 11.4 reduce-scatter.34.cloned.1.call-done
  1415.4 28.4 %reduce-scatter.32.cloned.1.call-done = f32[1728,72]{1,0:T(8,128)} async-done(((f32[3456,72]{1,0:T(8,128)}), f32[1728,72]{1,0:T(8,128)}) %reduce-scatter.32.cloned.1.call-update) | async-done | bytes 497680
  1443.8 1.6 copy.113
  1445.4 2.7 divide_subtract_fusion.3
  1448.2 21.8 %reduce-scatter.28.cloned.1.call-done = f32[72,2304]{1,0:T(8,128)} async-done(((f32[72,4608]{1,0:T(8,128)}), f32[72,2304]{1,0:T(8,128)}) %reduce-scatter.28.cloned.1.call-update) | async-done | bytes 663568 | tf_op jit(solution)/shard_map/reduce_scatter | solution.py:81
  1470.0 2.6 divide_subtract_fusion.2
  (287 shorter events, 45.3 us)
Async XLA Ops:
  7.2 117.8 %all-gather.12.cloned.1.call-start = ((), (), s32[]{:S(2)}) async-start(), calls=%async_computation.10 | async-start | bytes 8460288 | tf_op jit(solution)/shard_map/all_gather | solution.py:70
  20.0 132.9 %all-gather.14.cloned.1.call-start = ((), (), s32[]{:S(2)}) async-start(), calls=%async_computation.11 | async-start | bytes 2820096 | tf_op jit(solution)/shard_map/all_gather | solution.py:70
  26.4 201.6 %all-gather.16.cloned.1.call-start = ((), (), s32[]{:S(2)}) async-start(), calls=%async_computation.12 | async-start | bytes 11280384 | tf_op jit(solution)/shard_map/all_gather | solution.py:70
  26.6 84.1 %copy-start.62 = (f32[576]{0:T(1024)S(1)}, f32[576]{0:T(1024)}, u32[]{:S(2)}) copy-start(f32[576]{0:T(1024)} %param.49) | copy-start | bytes 6916
  26.6 92.1 %copy-start.41 = (f32[2304]{0:T(1024)S(1)}, f32[2304]{0:T(1024)}, u32[]{:S(2)}) copy-start(f32[2304]{0:T(1024)} %param.47) | copy-start | bytes 27652
  35.3 88.5 %copy-start = (f32[1,128,1152]{2,1,0:T(8,128)S(1)}, f32[1,128,1152]{2,1,0:T(8,128)}, u32[]{:S(2)}) copy-start(f32[1,128,1152]{2,1,0:T(8,128)} %param.35) | copy-start | bytes 1769476
  35.3 419.3 %reduce-scatter.30.cloned.1.call-start = ((), (), s32[]{:S(2)}) async-start(), calls=%async_computation.18 | async-start | bytes 22560768 | tf_op jit(solution)/shard_map/reduce_scatter | solution.py:80
  242.7 242.6 %reduce-scatter.36.cloned.1.call-start = ((), (), s32[]{:S(2)}) async-start(), calls=%async_computation.21 | async-start | bytes 2654208
  457.8 137.1 %all-gather.18.cloned.1.call-start = ((), (), s32[]{:S(2)}) async-start(), calls=%async_computation.13 | async-start | bytes 11280384 | tf_op jit(solution)/shard_map/all_gather | solution.py:70
  506.3 134.0 %reduce-scatter.24.cloned.1.call-start = ((), (), s32[]{:S(2)}) async-start(), calls=%async_computation.15 | async-start | bytes 1769472 | tf_op jit(solution)/shard_map/reduce_scatter | solution.py:229
  620.1 44.3 %reduce-scatter.22.cloned.1.call-start = ((), (), s32[]{:S(2)}) async-start(), calls=%async_computation.14 | async-start | bytes 1769472 | tf_op jit(solution)/shard_map/reduce_scatter | solution.py:228
  624.5 178.9 %all-reduce.13.cloned.1.call-start = ((), (), s32[]{:S(2)}) async-start(), calls=%async_computation.22 | async-start | bytes 442368
  671.3 134.2 %copy-start.6 = (f32[1,128,1152]{2,1,0:T(8,128)S(1)}, f32[1,128,1152]{2,1,0:T(8,128)}, u32[]{:S(2)}) copy-start(f32[1,128,1152]{2,1,0:T(8,128)} %copy-done.5) | copy-start | bytes 1769476
  678.5 152.5 %all-reduce.17.cloned.1.call-start = ((), (), s32[]{:S(2)}) async-start(), calls=%async_computation.26 | async-start | bytes 180224 | tf_op jit(solution)/shard_map/psum | solution.py:270
  805.5 107.4 %reduce-scatter.40.cloned.1.call-start = ((), (), s32[]{:S(2)}) async-start(), calls=%async_computation.24 | async-start | bytes 5640192
  809.7 276.8 %reduce-scatter.38.cloned.1.call-start = ((), (), s32[]{:S(2)}) async-start(), calls=%async_computation.23 | async-start | bytes 16920576
  818.8 484.4 %reduce-scatter.26.cloned.1.call-start = ((), (), s32[]{:S(2)}) async-start(), calls=%async_computation.16 | async-start | bytes 22560768 | tf_op jit(solution)/shard_map/reduce_scatter | solution.py:80
  830.9 564.0 %all-reduce.15.cloned.1.call-start = ((), (), s32[]{:S(2)}) async-start(), calls=%async_computation.25 | async-start | bytes 180224 | tf_op jit(solution)/shard_map/psum | solution.py:269
  831.5 581.8 %reduce-scatter.34.cloned.1.call-start = ((), (), s32[]{:S(2)}) async-start(), calls=%async_computation.20 | async-start | bytes 884736
  914.9 174.7 %copy-start.80 = (f32[128]{0:T(128)S(1)}, f32[128]{0:T(128)}, u32[]{:S(2)}) copy-start(f32[128]{0:T(128)} %get-tuple-element.46) | copy-start | bytes 1540
  914.9 174.7 %copy-start.81 = (f32[128]{0:T(128)S(1)}, f32[128]{0:T(128)}, u32[]{:S(2)}) copy-start(f32[128]{0:T(128)} %get-tuple-element.54) | copy-start | bytes 1540
  914.9 174.7 %copy-start.55 = (f32[128]{0:T(128)S(1)}, f32[128]{0:T(128)}, u32[]{:S(2)}) copy-start(f32[128]{0:T(128)} %copy-done.54) | copy-start | bytes 1540
  914.9 174.7 %copy-start.59 = (f32[128]{0:T(128)S(1)}, f32[128]{0:T(128)}, u32[]{:S(2)}) copy-start(f32[128]{0:T(128)} %copy-done.58) | copy-start | bytes 1540
  914.9 528.9 %reduce-scatter.32.cloned.1.call-start = ((), (), s32[]{:S(2)}) async-start(), calls=%async_computation.19 | async-start | bytes 2654208
  1089.4 213.8 %copy-start.77 = (f32[216]{0:T(256)S(1)}, f32[216]{0:T(256)}, u32[]{:S(2)}) copy-start(f32[216]{0:T(256)} %param.41) | copy-start | bytes 2596
  1089.4 213.8 %copy-start.78 = (f32[216]{0:T(256)S(1)}, f32[216]{0:T(256)}, u32[]{:S(2)}) copy-start(f32[216]{0:T(256)} %param.51) | copy-start | bytes 2596
  1089.4 213.8 %copy-start.79 = (f32[216]{0:T(256)S(1)}, f32[216]{0:T(256)}, u32[]{:S(2)}) copy-start(f32[216]{0:T(256)} %param.61) | copy-start | bytes 2596
  1089.4 214.4 %copy-start.13 = (f32[1152,216]{0,1:T(8,128)S(1)}, f32[1152,216]{0,1:T(8,128)}, u32[]{:S(2)}) copy-start(f32[1152,216]{0,1:T(8,128)} %param.40) | copy-start | bytes 2985988
  1089.4 214.4 %copy-start.35 = (bf16[8,1152]{1,0:T(8,128)(2,1)S(1)}, bf16[8,1152]{1,0:T(8,128)(2,1)}, u32[]{:S(2)}) copy-start(bf16[8,1152]{1,0:T(8,128)(2,1)} %copy-done.34) | copy-start | bytes 55300
  1089.5 380.5 %reduce-scatter.28.cloned.1.call-start = ((), (), s32[]{:S(2)}) async-start(), calls=%async_computation.17 | async-start | bytes 1990656 | tf_op jit(solution)/shard_map/reduce_scatter | solution.py:81
  1091.5 217.4 %copy-start.71 = (f32[216]{0:T(256)}, f32[216]{0:T(256)S(1)}, u32[]{:S(2)}) copy-start(f32[216]{0:T(256)S(1)} %dynamic-slice_reduce_fusion) | copy-start | bytes 2596
  1303.9 91.0 %copy-start.61 = (f32[576]{0:T(1024)S(1)}, f32[576]{0:T(1024)}, u32[]{:S(2)}) copy-start(f32[576]{0:T(1024)} %param.45) | copy-start | bytes 6916
  1303.9 91.1 %copy-start.72 = (f32[576]{0:T(1024)S(1)}, f32[576]{0:T(1024)}, u32[]{:S(2)}) copy-start(f32[576]{0:T(1024)} %param.55) | copy-start | bytes 6916
  1303.9 91.0 %copy-start.73 = (f32[576]{0:T(1024)S(1)}, f32[576]{0:T(1024)}, u32[]{:S(2)}) copy-start(f32[576]{0:T(1024)} %param.65) | copy-start | bytes 6916
  1303.9 92.4 %copy-start.63 = (f32[576]{0:T(1024)S(1)}, f32[576]{0:T(1024)}, u32[]{:S(2)}) copy-start(f32[576]{0:T(1024)} %param.49) | copy-start | bytes 6916
  1303.9 92.4 %copy-start.74 = (f32[576]{0:T(1024)S(1)}, f32[576]{0:T(1024)}, u32[]{:S(2)}) copy-start(f32[576]{0:T(1024)} %param.59) | copy-start | bytes 6916
  1303.9 92.4 %copy-start.75 = (f32[576]{0:T(1024)S(1)}, f32[576]{0:T(1024)}, u32[]{:S(2)}) copy-start(f32[576]{0:T(1024)} %param.69) | copy-start | bytes 6916
  1303.9 93.8 %copy-start.49 = (f32[1728]{0:T(1024)S(1)}, f32[1728]{0:T(1024)}, u32[]{:S(2)}) copy-start(f32[1728]{0:T(1024)} %param.43) | copy-start | bytes 20740
  1303.9 93.8 %copy-start.69 = (f32[1728]{0:T(1024)S(1)}, f32[1728]{0:T(1024)}, u32[]{:S(2)}) copy-start(f32[1728]{0:T(1024)} %param.53) | copy-start | bytes 20740
  1303.9 93.8 %copy-start.70 = (f32[1728]{0:T(1024)S(1)}, f32[1728]{0:T(1024)}, u32[]{:S(2)}) copy-start(f32[1728]{0:T(1024)} %param.63) | copy-start | bytes 20740
  1304.0 95.2 %copy-start.42 = (f32[2304]{0:T(1024)S(1)}, f32[2304]{0:T(1024)}, u32[]{:S(2)}) copy-start(f32[2304]{0:T(1024)} %param.47) | copy-start | bytes 27652
  1304.0 95.2 %copy-start.64 = (f32[2304]{0:T(1024)S(1)}, f32[2304]{0:T(1024)}, u32[]{:S(2)}) copy-start(f32[2304]{0:T(1024)} %param.57) | copy-start | bytes 27652
  1304.0 95.2 %copy-start.65 = (f32[2304]{0:T(1024)S(1)}, f32[2304]{0:T(1024)}, u32[]{:S(2)}) copy-start(f32[2304]{0:T(1024)} %param.67) | copy-start | bytes 27652
  1304.0 96.6 %copy-start.37 = (f32[8,1152]{1,0:T(8,128)S(1)}, f32[8,1152]{1,0:T(8,128)}, u32[]{:S(2)}) copy-start(f32[8,1152]{1,0:T(8,128)} %param.36) | copy-start | bytes 110596
  1304.0 110.5 %copy-start.24 = (f32[72,576]{1,0:T(8,128)S(1)}, f32[72,576]{1,0:T(8,128)}, u32[]{:S(2)}) copy-start(f32[72,576]{1,0:T(8,128)} %param.44) | copy-start | bytes 497668
  1304.0 110.4 %copy-start.32 = (f32[72,576]{1,0:T(8,128)S(1)}, f32[72,576]{1,0:T(8,128)}, u32[]{:S(2)}) copy-start(f32[72,576]{1,0:T(8,128)} %param.54) | copy-start | bytes 497668
  1304.0 110.4 %copy-start.33 = (f32[72,576]{1,0:T(8,128)S(1)}, f32[72,576]{1,0:T(8,128)}, u32[]{:S(2)}) copy-start(f32[72,576]{1,0:T(8,128)} %param.64) | copy-start | bytes 497668
  1308.9 136.5 %copy-start.21 = (f32[72,1728]{1,0:T(8,128)S(1)}, f32[72,1728]{1,0:T(8,128)}, u32[]{:S(2)}) copy-start(f32[72,1728]{1,0:T(8,128)} %param.42) | copy-start | bytes 1492996
  (55 other events, 784.1 us)
Sparse Core Ops, SparseCore 0:
  20.1 73.9 all-gather.11
  96.8 41.6 all-gather.13
  140.8 87.1 all-gather.15
  242.8 211.8 reduce-scatter.29
  457.9 27.3 reduce-scatter.35
  506.5 88.3 all-gather.17
  620.2 20.0 reduce-scatter.23
  642.6 21.8 reduce-scatter.21
  678.6 124.6 all-reduce.12
  808.1 22.3 all-reduce.16
  834.5 78.2 reduce-scatter.39
  916.8 169.5 reduce-scatter.37
  1090.5 212.6 reduce-scatter.25
  1307.1 87.7 all-reduce.14
  1397.6 15.7 reduce-scatter.33
  1415.5 28.3 reduce-scatter.31
  1446.5 23.4 reduce-scatter.27
